TPU v7x, 128 devices: a whole 4x4x4 slice. The times are simulated.
128 devices in a mesh: dp: 4 (over z_hi, core), seq: 32 (over x, y, z_lo).
Axes of the slice: x: 4, y: 4, z: 4 (z_hi: 2, z_lo: 2; z = z_hi * 2 + z_lo), core: 2. Of those that a mesh axis runs over, the one named last changes fastest.
Arguments:
- queries: bfloat16 [4, 4096, 1024], P('dp', 'seq'), may hold values from -40 to 40
- key_rows: bfloat16 [4, 4096, 1024], P('dp', 'seq'), may hold values from -9 to 9
- value_rows: bfloat16 [4, 4096, 1024], P('dp', 'seq'), may hold values from -6 to 6
- query_tangent: bfloat16 [4, 4096, 1024], P('dp', 'seq'), may hold values from -6 to 6
- key_tangent: bfloat16 [4, 4096, 1024], P('dp', 'seq'), may hold values from -6 to 6
- value_tangent: bfloat16 [4, 4096, 1024], P('dp', 'seq'), may hold values from -6 to 6
- out_weight: bfloat16 [1024, 2048], replicated, may hold values from -0.75 to 0.75
- upstream: bfloat16 [4, 4096, 2048], P('dp', 'seq'), may hold values from -6 to 6
Outputs:
- block_out: bfloat16 [4, 4096, 2048], P('dp', 'seq')
- tangent_out: bfloat16 [4, 4096, 2048], P('dp', 'seq')
- grad_weight: float32 [1024, 2048], P(('dp', 'seq'))
- grad_query: bfloat16 [4, 4096, 1024], P('dp', 'seq')
- grad_key: bfloat16 [4, 4096, 1024], P('dp', 'seq')
- grad_value: bfloat16 [4, 4096, 1024], P('dp', 'seq')
All inputs are finite; a program needn't handle non-finite values.
Results may differ from a plain program's by a relative error of at most 0.035.
Values may be sent and summed in bfloat16 or wider, within the bound.
No kernel may reach another device: no remote copies, remote signals or barrier semaphores. Data moves between devices by JAX's collectives and lax.ppermute only.
A program may use at most 192 MiB of HBM per device.

v0:
```python
import math

import jax
import jax.numpy as jnp
from jax import lax
from jax.sharding import PartitionSpec as P

HEADS = 8
HEAD_DIM = 128


def to_heads(matrix):
    return matrix.reshape(matrix.shape[0], HEADS, HEAD_DIM)


def per_device(
    queries, key_rows, value_rows, query_tangent, key_tangent, value_tangent, out_weight, upstream
):
    local_q = to_heads(queries[0])
    local_tq = to_heads(query_tangent[0])
    tokens = queries.shape[1]
    attn_width = queries.shape[2]
    full_len = tokens * lax.axis_size("seq")
    softmax_scale = HEAD_DIM ** (-0.5)
    head_zeros = jnp.zeros((HEADS, tokens), jnp.float32)
    acc_zeros = jnp.zeros((tokens, HEADS, HEAD_DIM), jnp.float32)
    run_max = jnp.full((HEADS, tokens), -jnp.inf, jnp.float32)
    run_sum = head_zeros
    run_tan = head_zeros
    acc_main = acc_zeros
    acc_tan = acc_zeros
    key_piece = lax.all_gather(key_rows[0], "seq", axis=0, tiled=True)
    value_piece = lax.all_gather(value_rows[0], "seq", axis=0, tiled=True)
    key_tan_piece = lax.all_gather(key_tangent[0], "seq", axis=0, tiled=True)
    value_tan_piece = lax.all_gather(value_tangent[0], "seq", axis=0, tiled=True)
    key_heads = to_heads(key_piece)
    value_heads = to_heads(value_piece)
    key_tan_heads = to_heads(key_tan_piece)
    value_tan_heads = to_heads(value_tan_piece)
    scores = (
        jnp.einsum("thd,shd->hts", local_q, key_heads, preferred_element_type=jnp.float32)
        * softmax_scale
    )
    tan_scores = (
        jnp.einsum("thd,shd->hts", local_tq, key_heads, preferred_element_type=jnp.float32)
        + jnp.einsum("thd,shd->hts", local_q, key_tan_heads, preferred_element_type=jnp.float32)
    ) * softmax_scale
    new_max = jnp.max(scores, axis=2)
    shrink = jnp.exp(run_max - new_max)
    exp_scores = jnp.exp(scores - new_max[:, :, None])
    weighted = exp_scores * tan_scores
    run_sum = run_sum * shrink + jnp.sum(exp_scores, axis=2)
    run_tan = run_tan * shrink + jnp.sum(weighted, axis=2)
    exp_low = exp_scores.astype(jnp.bfloat16)
    weighted_low = weighted.astype(jnp.bfloat16)
    shrink_rows = shrink.T[:, :, None]
    acc_main = acc_main * shrink_rows + jnp.einsum(
        "hts,shd->thd", exp_low, value_heads, preferred_element_type=jnp.float32
    )
    acc_tan = (
        acc_tan * shrink_rows
        + jnp.einsum("hts,shd->thd", weighted_low, value_heads, preferred_element_type=jnp.float32)
        + jnp.einsum("hts,shd->thd", exp_low, value_tan_heads, preferred_element_type=jnp.float32)
    )
    key_store = key_piece
    value_store = value_piece
    folded = (new_max, run_sum, run_tan, acc_main, acc_tan, key_store, value_store)
    run_max, run_sum, run_tan, acc_main, acc_tan, key_store, value_store = folded
    sum_rows = run_sum.T[:, :, None]
    attn_wide = acc_main / sum_rows
    attn = attn_wide.astype(jnp.bfloat16)
    tan_attn = ((acc_tan - attn_wide * run_tan.T[:, :, None]) / sum_rows).astype(jnp.bfloat16)
    log_total = run_max + jnp.log(run_sum)
    attn_flat = attn.reshape(tokens, attn_width)
    tan_flat = tan_attn.reshape(tokens, attn_width)
    block_wide = jnp.dot(attn_flat, out_weight, preferred_element_type=jnp.float32)
    tan_wide = jnp.dot(tan_flat, out_weight, preferred_element_type=jnp.float32)
    cotangent = (tan_wide + upstream[0].astype(jnp.float32)).astype(jnp.bfloat16)
    grad_attn = jnp.einsum(
        "te,ke->tk", cotangent, out_weight, preferred_element_type=jnp.float32
    ).astype(jnp.bfloat16)
    grad_factor = 1.0 / math.sqrt(lax.axis_size("dp") * full_len)
    grad_heads = to_heads(grad_attn)
    row_delta = jnp.einsum("thd,thd->ht", grad_heads, attn, preferred_element_type=jnp.float32)
    key_all = to_heads(key_store)
    value_all = to_heads(value_store)
    scores_all = (
        jnp.einsum("thd,shd->hts", local_q, key_all, preferred_element_type=jnp.float32)
        * softmax_scale
    )
    attn_prob = jnp.exp(scores_all - log_total[:, :, None])
    grad_prob = jnp.einsum(
        "thd,shd->hts", grad_heads, value_all, preferred_element_type=jnp.float32
    )
    grad_scores = (attn_prob * (grad_prob - row_delta[:, :, None])).astype(jnp.bfloat16)
    grad_query = (
        softmax_scale
        * jnp.einsum("hts,shd->thd", grad_scores, key_all, preferred_element_type=jnp.float32)
    ).astype(jnp.bfloat16)
    prob_low = attn_prob.astype(jnp.bfloat16)
    key_part = softmax_scale * jnp.einsum(
        "hts,thd->shd", grad_scores, local_q, preferred_element_type=jnp.float32
    )
    value_part = jnp.einsum(
        "hts,thd->shd", prob_low, grad_heads, preferred_element_type=jnp.float32
    )
    summed = lax.psum_scatter(
        jnp.concatenate(
            [
                key_part.reshape(tokens * lax.axis_size("seq"), attn_width),
                value_part.reshape(tokens * lax.axis_size("seq"), attn_width),
            ],
            axis=1,
        ).astype(jnp.bfloat16),
        "seq",
        scatter_dimension=0,
        tiled=True,
    ).astype(jnp.float32)
    grad_key = summed[:, :attn_width].astype(jnp.bfloat16)
    grad_value = summed[:, attn_width:].astype(jnp.bfloat16)
    grad_weight = lax.psum_scatter(
        grad_factor
        * jnp.einsum("tk,te->ke", attn_flat, cotangent, preferred_element_type=jnp.float32),
        ("dp", "seq"),
        scatter_dimension=0,
        tiled=True,
    )
    return (
        block_wide.astype(jnp.bfloat16)[None],
        tan_wide.astype(jnp.bfloat16)[None],
        grad_weight,
        grad_query.reshape(tokens, attn_width)[None],
        grad_key[None],
        grad_value[None],
    )


def solution(mesh):
    placed = (
        P("dp", "seq", None),
        P("dp", "seq", None),
        P("dp", "seq", None),
        P("dp", "seq", None),
        P("dp", "seq", None),
        P("dp", "seq", None),
        P(),
        P("dp", "seq", None),
    )
    return jax.shard_map(
        per_device,
        mesh=mesh,
        in_specs=placed,
        out_specs=(
            P("dp", "seq", None),
            P("dp", "seq", None),
            P(("dp", "seq"), None),
            P("dp", "seq", None),
            P("dp", "seq", None),
            P("dp", "seq", None),
        ),
        check_vma=False,
    )
```

profile of v0, /device:TPU:0, one launch (start us, length us, event | category | flops | bytes accessed | tf_op | source)
XLA Modules:
  0.0 1989.6 jit_solution(8101367012612386936)
XLA Ops:
  7.2 0.0 all-gather.11.cloned.1.call-start
  7.2 0.7 all-gather.11.cloned.1.call-update
  7.9 0.0 all-gather.9.cloned.1.call-start
  7.9 1.8 copy.27
  9.7 0.0 all-gather.9.cloned.1.call-update
  9.8 0.0 all-gather.13.cloned.1.call-start
  9.8 1.8 copy.33
  11.6 0.0 all-gather.15.cloned.1.call-start
  11.7 0.5 all-gather.15.cloned.1.call-update
  12.2 0.0 reduce-scatter.5.cloned.1.call-start
  12.3 1.1 copy.54
  13.4 1.0 copy.55
  14.4 187.6 %all-gather.11.cloned.1.call-done = bf16[1,4096,1024]{2,1,0:T(8,128)(2,1)} async-done(((bf16[1,128,1024]{2,1,0:T(8,128)(2,1)}), bf16[1,4096,1024]{2,1,0:T(8,128)(2,1)}) %all-gather.11.cloned.1.call-update) | async-done | bytes 8388624 | tf_op jit(solution)/shard_map/all_gather | solution.py:33
  202.0 11.5 copy.30
  213.5 224.9 %all-gather.9.cloned.1.call-done = bf16[1,4096,1024]{1,2,0:T(8,128)(2,1)} async-done(((bf16[1,128,1024]{1,2,0:T(8,128)(2,1)}), bf16[1,4096,1024]{1,2,0:T(8,128)(2,1)}) %all-gather.9.cloned.1.call-update) | async-done | bytes 8388624 | tf_op jit(solution)/shard_map/all_gather | solution.py:32
  438.3 11.5 multiply_reduce_fusion
  449.9 8.6 fusion.1
  458.5 11.5 fusion.42
  470.0 206.0 %all-gather.13.cloned.1.call-done = bf16[1,4096,1024]{1,2,0:T(8,128)(2,1)} async-done(((bf16[1,128,1024]{1,2,0:T(8,128)(2,1)}), bf16[1,4096,1024]{1,2,0:T(8,128)(2,1)}) %all-gather.13.cloned.1.call-update) | async-done | bytes 8388624 | tf_op jit(solution)/shard_map/all_gather | solution.py:34
  676.1 19.8 fusion.50
  695.8 8.2 fusion.27
  704.0 10.6 fusion.33
  714.6 152.3 %all-gather.15.cloned.1.call-done = bf16[1,4096,1024]{2,1,0:T(8,128)(2,1)} async-done(((bf16[1,128,1024]{2,1,0:T(8,128)(2,1)}), bf16[1,4096,1024]{2,1,0:T(8,128)(2,1)}) %all-gather.15.cloned.1.call-update) | async-done | bytes 8388624 | tf_op jit(solution)/shard_map/all_gather | solution.py:35
  866.9 11.3 copy.36
  878.2 10.3 fusion.39
  888.6 0.7 fusion.51
  889.3 1.6 fusion.31
  890.9 0.1 bitcast_convert_fusion
  891.0 0.2 copy.40
  891.2 12.5 fusion.9
  903.8 12.0 copy.42
  915.7 1.0 copy.53
  916.8 1.3 multiply_reduce_fusion.1
  918.0 10.9 multiply_convert_fusion.1
  929.0 5.7 multiply_convert_fusion
  934.7 11.9 copy.41
  946.7 13.8 pad_maximum_fusion
  960.5 0.0 reduce-scatter.5.cloned.1.call-update
  960.5 0.0 reduce-scatter.3.cloned.1.call-start
  960.5 4.5 convolution_multiply_fusion
  965.0 0.0 reduce-scatter.3.cloned.1.call-update
  965.0 8.5 fusion.30
  973.5 0.9 copy.43
  974.4 3.7 fusion.12
  978.1 0.9 convert_bitcast_fusion
  979.0 341.5 %reduce-scatter.5.cloned.1.call-done = bf16[128,2048]{1,0:T(8,128)(2,1)} async-done(((bf16[4096,2048]{1,0:T(8,128)(2,1)}), bf16[128,2048]{1,0:T(8,128)(2,1)}) %reduce-scatter.5.cloned.1.call-update) | async-done | bytes 524304 | tf_op jit(solution)/shard_map/reduce_scatter | solution.py:107
  1320.4 1.9 slice_bitcast_fusion
  1322.3 660.5 %reduce-scatter.3.cloned.1.call-done = f32[8,2048]{1,0:T(8,128)} async-done(((f32[1024,2048]{1,0:T(8,128)}), f32[8,2048]{1,0:T(8,128)}) %reduce-scatter.3.cloned.1.call-update) | async-done | bytes 65552 | tf_op jit(solution)/shard_map/reduce_scatter | solution.py:121
  (12 shorter events, 0.1 us)
Async XLA Ops:
  7.2 194.8 %all-gather.11.cloned.1.call-start = ((), (), s32[]{:S(2)}) async-start(), calls=%async_computation.5 | async-start | bytes 8650752 | tf_op jit(solution)/shard_map/all_gather | solution.py:33
  7.9 430.4 %all-gather.9.cloned.1.call-start = ((), (), s32[]{:S(2)}) async-start(), calls=%async_computation.4 | async-start | bytes 8650752 | tf_op jit(solution)/shard_map/all_gather | solution.py:32
  9.8 666.3 %all-gather.13.cloned.1.call-start = ((), (), s32[]{:S(2)}) async-start(), calls=%async_computation.6 | async-start | bytes 8650752 | tf_op jit(solution)/shard_map/all_gather | solution.py:34
  11.6 855.3 %all-gather.15.cloned.1.call-start = ((), (), s32[]{:S(2)}) async-start(), calls=%async_computation.7 | async-start | bytes 8650752 | tf_op jit(solution)/shard_map/all_gather | solution.py:35
  12.2 1308.2 %reduce-scatter.5.cloned.1.call-start = ((), (), s32[]{:S(2)}) async-start(), calls=%async_computation.3 | async-start | bytes 17301504 | tf_op jit(solution)/shard_map/reduce_scatter | solution.py:107
  714.6 163.6 %copy-start.3 = (f32[128,8,128]{0,2,1:T(8,128)}, f32[128,8,128]{0,2,1:T(8,128)S(1)}, u32[]{:S(2)}) copy-start(f32[128,8,128]{0,2,1:T(8,128)S(1)} %fusion.33) | copy-start | bytes 1572868
  878.2 10.3 copy-start.1
  878.2 11.1 copy-start.2
  929.0 5.7 copy-start
  960.5 1022.3 %reduce-scatter.3.cloned.1.call-start = ((), (), s32[]{:S(2)}) async-start(), calls=%async_computation.2 | async-start | bytes 8454144 | tf_op jit(solution)/shard_map/reduce_scatter | solution.py:121
Sparse Core Ops, SparseCore 0:
  9.6 192.2 all-gather.10
  204.1 234.1 all-gather.8
  440.5 235.5 all-gather.12
  677.6 189.2 all-gather.14
  960.6 359.7 reduce-scatter.4
  1323.2 659.4 reduce-scatter.2
where the time goes:
time: 1990 us
  waiting for transfers between devices  1770 us (89%)
  matrix products  120 us (6%)
  local copies, waits for them, and re-layouts  56.4 us (3%)
  other arithmetic  24.6 us (1%)
    reduce_scatter x1, waiting for transfers between devices, per_device(): lax.psum_scatter(grad_factor * jnp.einsum('tk,te->ke', attn_flat, cotange...  660 us
    reduce_scatter x1, waiting for transfers between devices, per_device(): lax.psum_scatter(jnp.concatenate([key_part.reshape(tokens * lax.axis_size...  341 us
    all_gather x1, waiting for transfers between devices, per_device(): key_piece = lax.all_gather(key_rows[0], 'seq', axis=0, tiled=True)  225 us
    all_gather x1, waiting for transfers between devices, per_device(): key_tan_piece = lax.all_gather(key_tangent[0], 'seq', axis=0, tiled=True)  206 us
    all_gather x1, waiting for transfers between devices, per_device(): value_piece = lax.all_gather(value_rows[0], 'seq', axis=0, tiled=True)  188 us
    all_gather x1, waiting for transfers between devices, per_device(): lax.all_gather(value_tangent[0], 'seq', axis=0, tiled=True)  152 us
  transfers between devices with their start and end apart: 6, of which 6 were waited for; matrix products, arithmetic and copies ran while one was open for 5% of the time, Pallas kernels for 0%

commit v1 on v0

v1 whole, which is shorter than its diff:
```python
import functools
import math

import jax
import jax.numpy as jnp
from jax import lax
from jax.experimental import pallas as pl
from jax.experimental.pallas import tpu as pltpu
from jax.sharding import Mesh
from jax.sharding import PartitionSpec as P

HEADS = 8
HEAD_DIM = 128
SCALE = HEAD_DIM**-0.5
LOG2E = math.log2(math.e)
SHAPE = (2, 2, 4, 4, 2)
NAMES = ("zh", "core", "x", "y", "zl")
SEQ = ("x", "y", "zl")
HEAD_AXES = ("y", "zl")
BF16 = jnp.bfloat16
F32 = jnp.float32
VMEM_LIMIT = 60 * 1024 * 1024

NT = (((1,), (1,)), ((), ()))
NN = (((1,), (0,)), ((), ()))
TN = (((0,), (0,)), ((), ()))


def dot(a, b, dims):
    return lax.dot_general(a, b, dims, preferred_element_type=F32)


def params(**kw):
    return pltpu.CompilerParams(vmem_limit_bytes=VMEM_LIMIT, **kw)


def split_kernel(k, v, tk, tv, q, tq, kv_out, q_out):
    for x in range(kv_out.shape[0]):
        for at, ref in enumerate((k, tk, v, tv)):
            kv_out[x, 0, at] = ref[...]
    for at, ref in enumerate((q, tq)):
        q_out[0, at] = ref[...]


def split_heads(k, v, tk, tv, q, tq, copies):
    tokens = k.shape[0]
    part = pl.BlockSpec((tokens, HEAD_DIM), lambda h: (0, h))
    return pl.pallas_call(
        split_kernel,
        grid=(HEADS,),
        in_specs=[part] * 6,
        out_specs=[
            pl.BlockSpec((copies, 1, 4, tokens, HEAD_DIM), lambda h: (0, h, 0, 0, 0)),
            pl.BlockSpec((1, 2, tokens, HEAD_DIM), lambda h: (h, 0, 0, 0)),
        ],
        out_shape=[
            jax.ShapeDtypeStruct((copies, HEADS, 4, tokens, HEAD_DIM), BF16),
            jax.ShapeDtypeStruct((HEADS, 2, tokens, HEAD_DIM), BF16),
        ],
        name="split_heads",
    )(k, v, tk, tv, q, tq)


def forward_kernel(kv, q, exp_out, out, attn_t_out, stats_out, kk, vt, s_scr, w_scr, *, chunk):
    keys = s_scr.shape[0]
    sources, tokens = kv.shape[0], kv.shape[2]
    rows = s_scr.shape[1]

    @pl.when(pl.program_id(0) == 0)
    def _():
        for s in range(sources):
            at = pl.ds(s * tokens, tokens)
            kk[at, :HEAD_DIM] = kv[s, 0]
            kk[at, HEAD_DIM:] = kv[s, 1]
            vt[:HEAD_DIM, s * tokens : (s + 1) * tokens] = kv[s, 2].T
            vt[HEAD_DIM:, s * tokens : (s + 1) * tokens] = kv[s, 3].T

    q_blk = q[:, 0].reshape(rows, HEAD_DIM)
    tq_blk = q[:, 1].reshape(rows, HEAD_DIM)
    both = jnp.concatenate([tq_blk, q_blk], axis=1)
    top = jnp.full((8, rows), -jnp.inf, F32)
    for c in range(keys // chunk):
        at = pl.ds(c * chunk, chunk)
        s = dot(kk[at, :HEAD_DIM], q_blk, NT)
        s_scr[at, :] = s
        top = jnp.maximum(top, jnp.max(s.reshape(chunk // 8, 8, rows), axis=0))
    top = jnp.max(top, axis=0, keepdims=True)
    total = jnp.zeros((8, rows), F32)
    tan_total = jnp.zeros((8, rows), F32)
    for c in range(keys // chunk):
        at = pl.ds(c * chunk, chunk)
        e = jnp.exp2((s_scr[at, :] - top) * (SCALE * LOG2E))
        w = e * dot(kk[at, :], both, NT)
        total += jnp.sum(e.reshape(chunk // 8, 8, rows), axis=0)
        tan_total += jnp.sum(w.reshape(chunk // 8, 8, rows), axis=0)
        exp_out[at, :] = e.astype(BF16)
        w_scr[at, :] = w.astype(BF16)
    total = jnp.sum(total, axis=0, keepdims=True)
    tan_total = jnp.sum(tan_total, axis=0, keepdims=True) * SCALE
    ev = dot(vt[...], exp_out[...], NN)
    wv = dot(vt[:HEAD_DIM, :], w_scr[...], NN)
    inv = 1.0 / total
    wide = ev[:HEAD_DIM] * inv
    tan = (wv * SCALE + ev[HEAD_DIM:] - wide * tan_total) * inv
    attn = wide.astype(BF16)
    attn_t_out[...] = attn
    stats_out[...] = jnp.broadcast_to(inv, stats_out.shape)
    per = rows // tokens
    out[:, 0] = attn.T.reshape(per, tokens, HEAD_DIM)
    out[:, 1] = tan.astype(BF16).T.reshape(per, tokens, HEAD_DIM)


def forward(kv, q, rows=256, chunk=512):
    sources, _, tokens, _ = kv.shape
    keys = sources * tokens
    groups = q.shape[0]
    queries = groups * tokens
    per = rows // tokens
    return pl.pallas_call(
        functools.partial(forward_kernel, chunk=chunk),
        grid=(queries // rows,),
        in_specs=[
            pl.BlockSpec(kv.shape, lambda i: (0, 0, 0, 0)),
            pl.BlockSpec((per, 2, tokens, HEAD_DIM), lambda i: (i, 0, 0, 0)),
        ],
        out_specs=[
            pl.BlockSpec((keys, rows), lambda i: (0, i)),
            pl.BlockSpec((per, 2, tokens, HEAD_DIM), lambda i: (i, 0, 0, 0)),
            pl.BlockSpec((HEAD_DIM, rows), lambda i: (0, i)),
            pl.BlockSpec((8, rows), lambda i: (0, i)),
        ],
        out_shape=[
            jax.ShapeDtypeStruct((keys, queries), BF16),
            jax.ShapeDtypeStruct((groups, 2, tokens, HEAD_DIM), BF16),
            jax.ShapeDtypeStruct((HEAD_DIM, queries), BF16),
            jax.ShapeDtypeStruct((8, queries), F32),
        ],
        scratch_shapes=[
            pltpu.VMEM((keys, 2 * HEAD_DIM), BF16),
            pltpu.VMEM((2 * HEAD_DIM, keys), BF16),
            pltpu.VMEM((keys, rows), F32),
            pltpu.VMEM((keys, rows), BF16),
        ],
        compiler_params=params(),
        name="forward",
    )(kv, q)


def project_kernel(x, w, up, tan_out, cot_out, grad_out, attn_out, tan_scr):
    for h in range(HEADS):
        at = slice(h * HEAD_DIM, (h + 1) * HEAD_DIM)
        attn_out[:, at] = x[h, 0]
        tan_scr[:, at] = x[h, 1]
    ty = dot(tan_scr[...], w[...], NN)
    tan_out[...] = ty.astype(BF16)
    cot = (ty + up[...].astype(F32)).astype(BF16)
    cot_out[...] = cot
    grad = dot(cot, w[...], NT).astype(BF16)
    for h in range(HEADS):
        grad_out[h] = grad[:, h * HEAD_DIM : (h + 1) * HEAD_DIM]


def project(x, w, up):
    tokens = up.shape[0]
    return pl.pallas_call(
        project_kernel,
        out_shape=[
            jax.ShapeDtypeStruct(up.shape, BF16),
            jax.ShapeDtypeStruct(up.shape, BF16),
            jax.ShapeDtypeStruct((HEADS, tokens, HEAD_DIM), BF16),
            jax.ShapeDtypeStruct((tokens, HEADS * HEAD_DIM), BF16),
        ],
        scratch_shapes=[pltpu.VMEM((tokens, HEADS * HEAD_DIM), BF16)],
        compiler_params=params(),
        name="project",
    )(x, w, up)


def backward_kernel(exp_t, kv, q, grad, attn_t, stats, dkv_out, dq_out, acc, delta):
    step = pl.program_id(0)
    per, tokens = kv.shape[0], kv.shape[2]
    block = per * tokens
    queries = exp_t.shape[1]
    g = grad[...].reshape(queries, HEAD_DIM)

    @pl.when(step == 0)
    def _():
        acc[...] = jnp.zeros_like(acc)
        both = g.astype(F32).T * attn_t[...].astype(F32)
        delta[...] = jnp.broadcast_to(jnp.sum(both, axis=0, keepdims=True), delta.shape)

    q_all = q[:, 0].reshape(queries, HEAD_DIM)
    k_blk = kv[:, 0].reshape(block, HEAD_DIM)
    v_blk = kv[:, 2].reshape(block, HEAD_DIM)
    prob = exp_t[...].astype(F32) * stats[:1, :]
    dp = dot(v_blk, g, NT)
    ds = (prob * (dp - delta[:1, :])).astype(BF16)
    dk = dot(ds, q_all, NN) * SCALE
    dv = dot(prob.astype(BF16), g, NN)
    dkv_out[:, 0] = dk.astype(BF16).reshape(per, tokens, HEAD_DIM)
    dkv_out[:, 1] = dv.astype(BF16).reshape(per, tokens, HEAD_DIM)
    acc[...] += dot(k_blk, ds, TN)

    @pl.when(step == pl.num_programs(0) - 1)
    def _():
        dq_out[...] = (acc[...] * SCALE).astype(BF16).T.reshape(dq_out.shape)


def backward(exp_t, kv, q, grad, attn_t, stats, block=512):
    sources, _, tokens, _ = kv.shape
    keys, queries = exp_t.shape
    per = block // tokens
    groups = q.shape[0]
    whole = lambda a: pl.BlockSpec(a.shape, lambda i: (0,) * a.ndim)
    return pl.pallas_call(
        backward_kernel,
        grid=(keys // block,),
        in_specs=[
            pl.BlockSpec((block, queries), lambda i: (i, 0)),
            pl.BlockSpec((per, 4, tokens, HEAD_DIM), lambda i: (i, 0, 0, 0)),
            whole(q),
            whole(grad),
            whole(attn_t),
            whole(stats),
        ],
        out_specs=[
            pl.BlockSpec((per, 2, tokens, HEAD_DIM), lambda i: (i, 0, 0, 0)),
            pl.BlockSpec((groups, tokens, HEAD_DIM), lambda i: (0, 0, 0)),
        ],
        out_shape=[
            jax.ShapeDtypeStruct((sources, 2, tokens, HEAD_DIM), BF16),
            jax.ShapeDtypeStruct((groups, tokens, HEAD_DIM), BF16),
        ],
        scratch_shapes=[
            pltpu.VMEM((HEAD_DIM, queries), F32),
            pltpu.VMEM((8, queries), F32),
        ],
        compiler_params=params(),
        name="backward",
    )(exp_t, kv, q, grad, attn_t, stats)


def join_kernel(dkv, dq, dk_out, dv_out, dq_out):
    terms = dkv[...].astype(F32)
    total = jnp.sum(terms, axis=0)[0]
    dk_out[...] = total[0].astype(BF16)
    dv_out[...] = total[1].astype(BF16)
    dq_out[...] = dq[0]


def join_heads(dkv, dq):
    copies, _, _, tokens, _ = dkv.shape
    part = pl.BlockSpec((tokens, HEAD_DIM), lambda h: (0, h))
    shape = jax.ShapeDtypeStruct((tokens, HEADS * HEAD_DIM), BF16)
    return pl.pallas_call(
        join_kernel,
        grid=(HEADS,),
        in_specs=[
            pl.BlockSpec((copies, 1, 2, tokens, HEAD_DIM), lambda h: (0, h, 0, 0, 0)),
            pl.BlockSpec((1, tokens, HEAD_DIM), lambda h: (h, 0, 0)),
        ],
        out_specs=[part] * 3,
        out_shape=[shape] * 3,
        name="join_heads",
    )(dkv, dq)


def exchange(value, axes):
    return lax.all_to_all(value, axes, 0, 0, tiled=True)


def weight_gradient(attn, cot):
    tokens, width = attn.shape
    core = lax.axis_index("core")
    swap = [(0, 1), (1, 0)]
    halves = attn.reshape(tokens, 2, 2, width // 4)
    lower, upper = halves[:, :, 0], halves[:, :, 1]
    mine = jnp.where(core == 0, lower, upper)
    theirs = lax.ppermute(jnp.where(core == 0, upper, lower), "core", swap)
    their_cot = lax.ppermute(cot, "core", swap)
    rows = jnp.concatenate([mine, theirs], axis=0).reshape(2 * tokens, width // 2)
    part = dot(rows, jnp.concatenate([cot, their_cot], axis=0), TN).astype(BF16)
    peers = lax.axis_size(("zh", "x", "y", "zl"))
    part = part.reshape(peers, width // (2 * peers), cot.shape[1])
    got = exchange(part, ("zh", "x", "y", "zl"))
    count = tokens * peers * 2
    return jnp.sum(got.astype(F32), axis=0) * (1.0 / math.sqrt(count))


def per_device(q, k, v, tq, tk, tv, weight, upstream):
    tokens, width = q.shape[1], q.shape[2]
    copies = lax.axis_size("x")
    kv_send, q_send = split_heads(k[0], v[0], tk[0], tv[0], q[0], tq[0], copies)
    q_all = exchange(q_send, HEAD_AXES)
    kv_all = exchange(kv_send.reshape(copies * HEADS, 4, tokens, HEAD_DIM), SEQ)
    exp_t, heads_out, attn_t, stats = forward(kv_all, q_all)
    owned = exchange(heads_out, HEAD_AXES)
    tan_out, cot, grad_send, attn = project(owned, weight, upstream[0])
    grad = exchange(grad_send, HEAD_AXES)
    block_out = dot(attn, weight, NN).astype(BF16)
    grad_weight = weight_gradient(attn, cot)
    dkv, dq = backward(exp_t, kv_all, q_all, grad, attn_t, stats)
    dq_all = exchange(dq, HEAD_AXES)
    dkv_all = exchange(dkv, SEQ).reshape(copies, HEADS, 2, tokens, HEAD_DIM)
    grad_key, grad_value, grad_query = join_heads(dkv_all, dq_all)
    return (
        block_out[None],
        tan_out[None],
        grad_weight,
        grad_query[None],
        grad_key[None],
        grad_value[None],
    )


def solution(mesh):
    parts = Mesh(mesh.devices.reshape(SHAPE), NAMES)
    tokens = P(("zh", "core"), SEQ, None)
    return jax.shard_map(
        per_device,
        mesh=parts,
        in_specs=(tokens,) * 6 + (P(), tokens),
        out_specs=(tokens, tokens, P(("zh", "core") + SEQ, None), tokens, tokens, tokens),
        check_vma=False,
    )
```

time: 1990 us -> 216 us (0.11)
  waiting for transfers between devices: 1770 us -> 36.1 us
  matrix products: 120 us -> 6.79 us
  blocking collectives: 0 us -> 106 us
  local copies, waits for them, and re-layouts: 56.4 us -> 0.69 us
  Pallas kernels: 0 us -> 47.3 us
  other arithmetic: 24.6 us -> 2.6 us
    reduce_scatter x2 -> x0, waiting for transfers between devices: 1000 us -> none  [the longest x1 660 us: per_device(): lax.psum_scatter(grad_factor * jnp.einsum('tk,te->ke', attn_flat, cotange...]
    all_gather x4 -> x0, waiting for transfers between devices: 771 us -> none  [the longest x1 225 us: per_device(): key_piece = lax.all_gather(key_rows[0], 'seq', axis=0, tiled=True)]
    dot_general x14 -> x2, matrix products: 120 us -> 6.79 us  [dot(): return lax.dot_general(a, b, dims, preferred_element_type=F32)]
    all_to_all x0 -> x5, blocking collectives: none -> 106 us  [exchange(): return lax.all_to_all(value, axes, 0, 0, tiled=True)]
    pallas_call x0 -> x5, Pallas kernels: none -> 47.3 us  [the longest x1 17.5 us: forward(): pl.pallas_call(functools.partial(forward_kernel, chunk=chunk), grid=(quer...]
    all_to_all x0 -> x2, waiting for transfers between devices: none -> 35 us  [exchange(): return lax.all_to_all(value, axes, 0, 0, tiled=True)]
    reshape x3 -> x1, local copies, waits for them, and re-layouts: 24.1 us -> 0.18 us  [weight_gradient(): halves = attn.reshape(tokens, 2, 2, width // 4)]
    all_gather x2 -> x0, local copies, waits for them, and re-layouts: 22.8 us -> none  [the longest x1 11.5 us: per_device(): value_piece = lax.all_gather(value_rows[0], 'seq', axis=0, tiled=True)]
  transfers between devices with their start and end apart: 6 -> 4, of which waited for: 6 -> 3; matrix products, arithmetic and copies ran while one was open for 5% -> 4% of each run, Pallas kernels for 0% -> 3%
where the time goes in v1:
time: 216 us; the launch traced here: 214 us
  blocking collectives  106 us (49%)
  Pallas kernels  47.3 us (22%)
  waiting for transfers between devices  36.1 us (17%)
  starting transfers between devices  13.1 us (6%)
  matrix products  6.79 us (3%)
  other arithmetic  2.6 us (1%)
    all_to_all x5, blocking collectives, exchange(): return lax.all_to_all(value, axes, 0, 0, tiled=True)  106 us
    all_to_all x2, waiting for transfers between devices, exchange(): return lax.all_to_all(value, axes, 0, 0, tiled=True)  35 us
    pallas_call x1, Pallas kernels, forward(): pl.pallas_call(functools.partial(forward_kernel, chunk=chunk), grid=(quer...  17.5 us
    pallas_call x1, Pallas kernels, backward(): pl.pallas_call(backward_kernel, grid=(keys // block,), in_specs=[pl.Block...  13.3 us
    all_to_all x2, starting transfers between devices, exchange(): return lax.all_to_all(value, axes, 0, 0, tiled=True)  12.4 us
    dot_general x2, matrix products, dot(): return lax.dot_general(a, b, dims, preferred_element_type=F32)  6.79 us
    pallas_call x1, Pallas kernels, split_heads(): pl.pallas_call(split_kernel, grid=(HEADS,), in_specs=[part] * 6, out_spec...  5.85 us
    pallas_call x1, Pallas kernels, join_heads(): pl.pallas_call(join_kernel, grid=(HEADS,), in_specs=[pl.BlockSpec((copies...  5.35 us
  transfers between devices with their start and end apart: 4, of which 3 were waited for; matrix products, arithmetic and copies ran while one was open for 4% of the time, Pallas kernels for 3%

profile of v1, /device:TPU:0, one launch (start us, length us, event | category | flops | bytes accessed | tf_op | source)
XLA Modules:
  0.0 213.7 jit_solution(12776128096654916380)
XLA Ops:
  0.6 5.8 %split_heads.1 = (bf16[4,8,4,128,128]{4,3,2,1,0:T(8,128)(2,1)}, bf16[8,2,128,128]{3,2,1,0:T(8,128)(2,1)}) custom-call(bf16[128,1024]{1,0:T(8,128)(2,1)} %bitcast.29, bf16[128,1024]{1,0:T(8,128)(2,1)} %bitcast.30, bf16[128,1024]{1,0:T(8,128)(2,1)} %bitcast.31, bf16[128,1024]{1,0:T(8,128)(2,1)} %bitcast.32, bf16[128,1024]{1,0:T(8,128)(2,1)} %bitcast.33, ...), custom_call_target="tpu_custom_call" | custom-call | tf_op jit(solution)/shard_map/split_heads/pallas_call | solution.py:48
  6.5 15.8 %all_to_all.35.q = bf16[8,2,128,128]{3,2,1,0:T(8,128)(2,1)} all-to-all(bf16[8,2,128,128]{3,2,1,0:T(8,128)(2,1)} %get-tuple-element.22), channel_id=1, replica_groups=mesh['zh'=2,'core'=2,'x'=4,'y'=4,'zl'=2] {'y','zl'}, dimensions={0} | all-to-all | bytes 1048576 | tf_op jit(solution)/shard_map/all_to_all | solution.py:269
  22.3 56.1 %all_to_all.36.kv = bf16[32,4,128,128]{3,2,1,0:T(8,128)(2,1)} all-to-all(bf16[32,4,128,128]{3,2,1,0:T(8,128)(2,1)} %bitcast.26), channel_id=1, replica_groups=mesh['zh'=2,'core'=2,'x'=4,'y'=4,'zl'=2] {'x','y','zl'}, dimensions={0} | all-to-all | bytes 8388608 | tf_op jit(solution)/shard_map/all_to_all | solution.py:269
  78.3 17.5 %forward.1 = (bf16[4096,1024]{1,0:T(8,128)(2,1)}, bf16[8,2,128,128]{3,2,1,0:T(8,128)(2,1)}, bf16[128,1024]{1,0:T(8,128)(2,1)}, f32[8,1024]{1,0:T(8,128)}) custom-call(bf16[32,4,128,128]{3,2,1,0:T(8,128)(2,1)} %all_to_all.36.kv, bf16[8,2,128,128]{3,2,1,0:T(8,128)(2,1)} %all_to_all.35.q), custom_call_target="tpu_custom_call" | custom-call | tf_op jit(solution)/shard_map/forward/pallas_call | solution.py:119
  95.9 12.5 %all_to_all.37.x = bf16[8,2,128,128]{3,2,1,0:T(8,128)(2,1)} all-to-all(bf16[8,2,128,128]{3,2,1,0:T(8,128)(2,1)} %get-tuple-element.23), channel_id=1, replica_groups=mesh['zh'=2,'core'=2,'x'=4,'y'=4,'zl'=2] {'y','zl'}, dimensions={0} | all-to-all | bytes 1048576 | tf_op jit(solution)/shard_map/all_to_all | solution.py:269
  108.4 5.3 %project.1 = (bf16[128,2048]{1,0:T(8,128)(2,1)}, bf16[128,2048]{1,0:T(8,128)(2,1)}, bf16[8,128,128]{2,1,0:T(8,128)(2,1)}, bf16[128,1024]{1,0:T(8,128)(2,1)}) custom-call(bf16[8,2,128,128]{3,2,1,0:T(8,128)(2,1)} %all_to_all.37.x, bf16[1024,2048]{1,0:T(8,128)(2,1)} %w.1, bf16[128,2048]{1,0:T(8,128)(2,1)} %bitcast.28), custom_call_target="tpu_custom_call" | custom-call | tf_op jit(solution)/shard_map/project/pallas_call | solution.py:165
  113.6 11.0 %all_to_all.38.grad = bf16[8,128,128]{2,1,0:T(8,128)(2,1)} all-to-all(bf16[8,128,128]{2,1,0:T(8,128)(2,1)} %get-tuple-element.28), channel_id=1, replica_groups=mesh['zh'=2,'core'=2,'x'=4,'y'=4,'zl'=2] {'y','zl'}, dimensions={0} | all-to-all | bytes 524288 | tf_op jit(solution)/shard_map/all_to_all | solution.py:269
  124.6 13.3 %backward.1 = (bf16[32,2,128,128]{3,2,1,0:T(8,128)(2,1)}, bf16[8,128,128]{2,1,0:T(8,128)(2,1)}) custom-call(bf16[4096,1024]{1,0:T(8,128)(2,1)} %get-tuple-element.27.exp_t, bf16[32,4,128,128]{3,2,1,0:T(8,128)(2,1)} %all_to_all.36.kv, bf16[8,2,128,128]{3,2,1,0:T(8,128)(2,1)} %all_to_all.35.q, bf16[8,128,128]{2,1,0:T(8,128)(2,1)} %all_to_all.38.grad, ...), custom_call_target="tpu_custom_call" | custom-call | tf_op jit(solution)/shard_map/backward/pallas_call | solution.py:215
  137.9 0.0 copy-start.1
  137.9 0.0 copy-start.2
  137.9 11.1 %all_to_all.39.dq = bf16[8,128,128]{2,1,0:T(8,128)(2,1)} all-to-all(bf16[8,128,128]{2,1,0:T(8,128)(2,1)} %get-tuple-element.32), channel_id=1, replica_groups=mesh['zh'=2,'core'=2,'x'=4,'y'=4,'zl'=2] {'y','zl'}, dimensions={0} | all-to-all | bytes 524288 | tf_op jit(solution)/shard_map/all_to_all | solution.py:269
  149.0 4.2 %all-to-all-start.5 = ((bf16[32,2,128,128]{3,2,1,0:T(8,128)(2,1)}), bf16[32,2,128,128]{3,2,1,0:T(8,128)(2,1)S(1)}, u32[]{:S(2)}, u32[]{:S(2)}) async-start(bf16[32,2,128,128]{3,2,1,0:T(8,128)(2,1)} %get-tuple-element.31), calls=%async_computation.5 | async-start | bytes 4194304 | tf_op jit(solution)/shard_map/all_to_all | solution.py:269
  153.2 0.0 copy-done.1
  153.3 0.2 reshape.32
  153.4 0.0 copy-done.2
  153.5 0.1 collective-permute-start.1
  153.5 0.4 fusion.6
  154.0 0.6 collective-permute-start
  154.5 1.1 collective-permute-done
  155.7 0.1 copy.22
  155.8 0.0 collective-permute-done.1
  155.8 3.1 %fusion = bf16[64,8,2048]{2,1,0:T(8,128)(2,1)} fusion(bf16[256,512]{0,1:T(8,128)(2,1)S(1)} %bitcast.27, bf16[128,2048]{1,0:T(8,128)(2,1)} %collective-permute-done.1, bf16[128,2048]{1,0:T(8,128)(2,1)S(1)} %copy-done.2), kind=kOutput, calls=%fused_computation.2 | convolution fusion | flops 540016640 | bytes 3407872 | tf_op jit(solution)/shard_map/dot_general | solution.py:30
  158.9 17.4 %all-to-all-done.5 = bf16[32,2,128,128]{3,2,1,0:T(8,128)(2,1)S(1)} async-done(((bf16[32,2,128,128]{3,2,1,0:T(8,128)(2,1)}), bf16[32,2,128,128]{3,2,1,0:T(8,128)(2,1)S(1)}, u32[]{:S(2)}, u32[]{:S(2)}) %all-to-all-start.5) | async-done | bytes 2097184 | tf_op jit(solution)/shard_map/all_to_all | solution.py:269
  176.3 0.0 copy-start
  176.3 8.2 %all-to-all-start.3 = ((bf16[64,8,2048]{2,1,0:T(8,128)(2,1)}), bf16[64,8,2048]{2,1,0:T(8,128)(2,1)}, u32[]{:S(2)}, u32[]{:S(2)}) async-start(bf16[64,8,2048]{2,1,0:T(8,128)(2,1)} %fusion), calls=%async_computation.3 | async-start | bytes 4194304 | tf_op jit(solution)/shard_map/all_to_all | solution.py:269
  184.5 3.7 %fusion.1 = bf16[1,128,2048]{2,1,0:T(8,128)(2,1)} fusion(bf16[128,1024]{1,0:T(8,128)(2,1)S(1)} %copy-done.1, bf16[1024,2048]{1,0:T(8,128)(2,1)} %w.1), kind=kOutput, calls=%fused_computation.4 | convolution fusion | flops 537133056 | bytes 4980736 | tf_op jit(solution)/shard_map/dot_general | solution.py:30
  188.2 0.0 copy-done
  188.2 5.4 %join_heads.1 = (bf16[128,1024]{1,0:T(8,128)(2,1)}, bf16[128,1024]{1,0:T(8,128)(2,1)}, bf16[128,1024]{1,0:T(8,128)(2,1)}) custom-call(bf16[4,8,2,128,128]{4,3,2,1,0:T(8,128)(2,1)} %bitcast.25, bf16[8,128,128]{2,1,0:T(8,128)(2,1)} %all_to_all.39.dq), custom_call_target="tpu_custom_call" | custom-call | tf_op jit(solution)/shard_map/join_heads/pallas_call | solution.py:255
  193.5 17.6 %all-to-all-done.3 = bf16[64,8,2048]{2,1,0:T(8,128)(2,1)} async-done(((bf16[64,8,2048]{2,1,0:T(8,128)(2,1)}), bf16[64,8,2048]{2,1,0:T(8,128)(2,1)}, u32[]{:S(2)}, u32[]{:S(2)}) %all-to-all-start.3) | async-done | bytes 2097184 | tf_op jit(solution)/shard_map/all_to_all | solution.py:269
  211.1 1.9 convert_reduce_fusion
  213.0 0.6 broadcast_multiply_fusion
  (2 shorter events, 0.1 us)
Async XLA Ops:
  137.9 15.4 %copy-start.1 = (bf16[128,1024]{1,0:T(8,128)(2,1)S(1)}, bf16[128,1024]{1,0:T(8,128)(2,1)}, u32[]{:S(2)}) copy-start(bf16[128,1024]{1,0:T(8,128)(2,1)} %get-tuple-element.24) | copy-start | bytes 786436
  137.9 15.6 %copy-start.2 = (bf16[128,2048]{1,0:T(8,128)(2,1)S(1)}, bf16[128,2048]{1,0:T(8,128)(2,1)}, u32[]{:S(2)}) copy-start(bf16[128,2048]{1,0:T(8,128)(2,1)} %get-tuple-element.26) | copy-start | bytes 1572868
  149.0 27.3 %all-to-all-start.5 = ((bf16[32,2,128,128]{3,2,1,0:T(8,128)(2,1)}), bf16[32,2,128,128]{3,2,1,0:T(8,128)(2,1)S(1)}, u32[]{:S(2)}, u32[]{:S(2)}) async-start(bf16[32,2,128,128]{3,2,1,0:T(8,128)(2,1)} %get-tuple-element.31), calls=%async_computation.5 | async-start | bytes 4194304 | tf_op jit(solution)/shard_map/all_to_all | solution.py:269
  153.5 2.3 %collective-permute-start.1 = (bf16[128,2048]{1,0:T(8,128)(2,1)S(1)}, bf16[128,2048]{1,0:T(8,128)(2,1)}, u32[]{:S(2)}, u32[]{:S(2)}) collective-permute-start(bf16[128,2048]{1,0:T(8,128)(2,1)S(1)} %copy-done.2), channel_id=1, source_target_pairs={{0,32},{32,0},{1,33},{33,1},{2,34},{34,2},{3,35},{35,3},{4,36},{36... | collective-permute-start | bytes 1572872 | tf_op jit(solution)/shard_map/ppermute | solution.py:280
  154.0 1.7 collective-permute-start
  176.3 11.9 %copy-start = (bf16[32,2,128,128]{3,2,1,0:T(8,128)(2,1)}, bf16[32,2,128,128]{3,2,1,0:T(8,128)(2,1)S(1)}, u32[]{:S(2)}) copy-start(bf16[32,2,128,128]{3,2,1,0:T(8,128)(2,1)S(1)} %all-to-all-done.5) | copy-start | bytes 6291460
  176.3 34.8 %all-to-all-start.3 = ((bf16[64,8,2048]{2,1,0:T(8,128)(2,1)}), bf16[64,8,2048]{2,1,0:T(8,128)(2,1)}, u32[]{:S(2)}, u32[]{:S(2)}) async-start(bf16[64,8,2048]{2,1,0:T(8,128)(2,1)} %fusion), calls=%async_computation.3 | async-start | bytes 4194304 | tf_op jit(solution)/shard_map/all_to_all | solution.py:269
